TPU v7x, 512 devices: a whole 4x4x16 slice. The times are simulated.
512 devices in a mesh: space: 32 (over z, x_lo), field: 16 (over x_hi, y, core).
Axes of the slice: x: 4 (x_hi: 2, x_lo: 2; x = x_hi * 2 + x_lo), y: 4, z: 16, core: 2. Of those that a mesh axis runs over, the one named last changes fastest.
Arguments:
- composition_vector: float32 [16, 32, 128, 16, 128], P('field', None, 'space'), may hold values from -6 to 6
- filtered_motion: float32 [3, 128, 16, 128], P(None, 'space', 'field'), may hold values from -1.8 to 1.8
- spreading_strength: float32 [128, 16, 128], P('space', 'field'), may hold values from 0.02 to 0.12
- blend_relax_multiplier: float32 [128, 16, 128], P('space', 'field'), may hold values from 0.2 to 0.9
- thermal_level: float32 [128, 16, 128], P('space', 'field'), may hold values from 0.5 to 2
- brownian_jumps: float32 [2, 16, 3], P(None, 'field'), may hold values from -2.5 to 2.5
- left_bilinear_weights: bfloat16 [206, 32], replicated, may hold values from -1 to 1
- right_bilinear_weights: bfloat16 [206, 32], replicated, may hold values from -1 to 1
- species_yield_weights: bfloat16 [32, 206], replicated, may hold values from -0.4375 to 0.4375
- arrhenius_prefactor: float32 [206], replicated, may hold values from 0.3 to 3
- ignition_energy_ratio: float32 [206], replicated, may hold values from 0.2 to 2
Outputs:
- result: float32 [16, 32, 128, 16, 128], P('field', None, 'space')
All inputs are finite; a program needn't handle non-finite values.
Results may differ from a plain program's by a relative error of at most 0.00068.
Values sent between devices are 32-bit elements; how exact they have to be, the bound alone decides.
No kernel may reach another device: no remote copies, remote signals or barrier semaphores. Data moves between devices by JAX's collectives and lax.ppermute only.
A program may use at most 64 MiB of HBM per device.

v0:
```python
import jax
import jax.numpy as jnp
from jax import lax
from jax.sharding import PartitionSpec as P

STEPS = 2
SUB = 5
chem_step = 0.2


def turned_gather(arrays, axis, dims):
    turned = [jnp.moveaxis(a, dim, 0) for a, dim in zip(arrays, dims)]
    widths = [t[0].size for t in turned]
    both = jnp.concatenate([t.reshape(-1, w) for t, w in zip(turned, widths)], axis=1)
    result = lax.all_gather(both, axis, axis=0, tiled=True)
    tiles = jnp.split(result, [sum(widths[:k]) for k in range(1, len(widths))], axis=1)
    return tuple(
        (
            jnp.moveaxis(b.reshape(-1, *t.shape[1:]), 0, dim)
            for b, t, dim in zip(tiles, turned, dims)
        )
    )


def split_up(value, dim, count):
    dims = value.shape
    tiles = value.reshape(*dims[:dim], count, dims[dim] // count, *dims[dim + 1 :])
    return jnp.moveaxis(tiles, dim, 0)


def sent_and_summed(value, axis, dim):
    tiles = split_up(value, dim, lax.axis_size(axis))
    arrived = lax.all_to_all(tiles, axis, split_axis=0, concat_axis=0, tiled=True)
    return arrived.sum(axis=0)


def laid_out(tiles, dim):
    dims = list(tiles.shape[1:])
    dims[dim] *= tiles.shape[0]
    return jnp.moveaxis(tiles, 0, dim).reshape(dims)


def from_everyone(value, axis):
    count = lax.axis_size(axis)
    return lax.all_to_all(
        jnp.broadcast_to(value[None], (count, *value.shape)), axis, 0, 0, tiled=True
    )


def collect(value, axis, dim):
    return laid_out(from_everyone(value, axis), dim)


def extended(value, sides, width):
    for axis, dim in sides:
        count, length = (lax.axis_size(axis), value.shape[dim])
        up = [(i, (i + 1) % count) for i in range(count)]
        down = [(j, i) for i, j in up]
        last = lax.slice_in_dim(value, length - width, length, axis=dim)
        leading = lax.slice_in_dim(value, 0, width, axis=dim)
        before = lax.ppermute(last, axis, up)
        after = lax.ppermute(leading, axis, down)
        value = jnp.concatenate([before, value, after], axis=dim)
    return value


def transport(padded, current, mean, filtered_motion, spreading_strength, mixing, wiener):
    x_plus = padded[:, 2:]
    x_minus = padded[:, :-2]
    y_plus = jnp.roll(current, -1, 2)
    y_minus = jnp.roll(current, 1, 2)
    z_plus = jnp.roll(current, -1, 3)
    z_minus = jnp.roll(current, 1, 3)
    grad_x = 0.5 * (x_plus - x_minus)
    grad_y = 0.5 * (y_plus - y_minus)
    grad_z = 0.5 * (z_plus - z_minus)
    laplace = x_plus + x_minus + y_plus + y_minus + z_plus + z_minus - 6.0 * current
    advect = filtered_motion[0] * grad_x + filtered_motion[1] * grad_y + filtered_motion[2] * grad_z
    noise = jnp.sqrt(2.0 * spreading_strength) * (
        wiener[0] * grad_x + wiener[1] * grad_y + wiener[2] * grad_z
    )
    return current - advect + spreading_strength * laplace + noise - mixing * (current - mean)


def react(block, arrhenius, left_bilinear_weights, right_bilinear_weights, species_yield_weights):
    for substep in range(SUB):
        lowered = block.astype(jnp.bfloat16)
        forward = jnp.dot(left_bilinear_weights, lowered, preferred_element_type=jnp.float32)
        backward = jnp.dot(right_bilinear_weights, lowered, preferred_element_type=jnp.float32)
        saturation = 1.0 + forward * forward + backward * backward
        rates = (arrhenius * forward * backward / saturation).astype(jnp.bfloat16)
        block = block + chem_step * jnp.dot(
            species_yield_weights, rates, preferred_element_type=jnp.float32
        )
    return block


def kinetic_yield_term(
    carried_ensemble,
    thermal_level,
    arrhenius_prefactor,
    ignition_energy_ratio,
    left_bilinear_weights,
    right_bilinear_weights,
    species_yield_weights,
):
    species_count, planes, vertical_extent, streamwise_extent = carried_ensemble.shape

    def one_plane(plane_index, current):
        starting_ensemble = jnp.asarray(plane_index).astype(jnp.int32)
        block = lax.dynamic_slice_in_dim(current, starting_ensemble, 1, 1).reshape(
            species_count, vertical_extent * streamwise_extent
        )
        enthalpy_output = lax.dynamic_slice_in_dim(thermal_level, starting_ensemble, 1, 0).reshape(
            1, vertical_extent * streamwise_extent
        )
        arrhenius = arrhenius_prefactor[:, None] * jnp.exp(
            -ignition_energy_ratio[:, None] / enthalpy_output
        )
        reacted = react(
            block, arrhenius, left_bilinear_weights, right_bilinear_weights, species_yield_weights
        )
        reacted = reacted.reshape(species_count, 1, vertical_extent, streamwise_extent)
        return lax.dynamic_update_slice_in_dim(current, reacted, starting_ensemble, 1)

    return lax.fori_loop(0, planes, one_plane, carried_ensemble)


def body(
    composition_vector,
    filtered_motion,
    spreading_strength,
    blend_relax_multiplier,
    thermal_level,
    brownian_jumps,
    left_bilinear_weights,
    right_bilinear_weights,
    species_yield_weights,
    arrhenius_prefactor,
    ignition_energy_ratio,
):
    fields = lax.axis_size("field")
    motion_lookup, spreading_gradient_sum, subgrid_blend_sum, thermal_lookup = turned_gather(
        (filtered_motion, spreading_strength, blend_relax_multiplier, thermal_level),
        "field",
        (2, 1, 1, 1),
    )
    current = composition_vector[0]
    for step in range(STEPS):
        share = sent_and_summed(current, "field", 2) / fields
        mean = collect(share, "field", 2)
        padded = extended(current, (("space", 1),), 1)
        carried_ensemble = transport(
            padded,
            current,
            mean,
            motion_lookup,
            spreading_gradient_sum,
            subgrid_blend_sum,
            brownian_jumps[step, 0],
        )
        current = kinetic_yield_term(
            carried_ensemble,
            thermal_lookup,
            arrhenius_prefactor,
            ignition_energy_ratio,
            left_bilinear_weights,
            right_bilinear_weights,
            species_yield_weights,
        )
    return current[None]


def solution(mesh):
    return jax.shard_map(
        body,
        mesh=mesh,
        in_specs=(
            P("field", None, "space", None, None),
            P(None, "space", "field", None),
            P("space", "field", None),
            P("space", "field", None),
            P("space", "field", None),
            P(None, "field", None),
            P(),
            P(),
            P(),
            P(),
            P(),
        ),
        out_specs=P("field", None, "space", None, None),
        check_vma=False,
    )
```

profile of v0, /device:TPU:6, one launch (start us, length us, event | category | flops | bytes accessed | tf_op | source)
XLA Modules:
  0.0 205.6 jit_solution(5558131106530953683)
XLA Ops:
  0.0 2.7 %copy.133 = f32[1,32,4,16,128]{4,2,1,3,0:T(4,128)} copy(f32[1,32,4,16,128]{4,3,2,1,0:T(8,128)} %param.15) | data formatting | bytes 2097152 | tf_op args[0]
  2.7 7.5 %all-to-all-start = ((f32[16,32,4,1,128]{4,2,1,3,0:T(4,128)}), f32[16,32,4,1,128]{4,2,1,3,0:T(4,128)S(1)}, u32[]{:S(2)}, u32[]{:S(2)}) async-start(f32[16,32,4,1,128]{4,2,1,3,0:T(4,128)} %bitcast.249), calls=%async_computation | async-start | bytes 2097152 | tf_op jit(solution)/shard_map/all_to_all | solution.py:33
  11.7 4.6 %collective-permute-start = (f32[32,1,16,128]{3,0,1,2:T(8,128)}, f32[32,1,16,128]{3,0,1,2:T(8,128)}, u32[]{:S(2)}, u32[]{:S(2)}) collective-permute-start(f32[32,1,16,128]{3,0,1,2:T(8,128)} %get-tuple-element.496), channel_id=1, source_target_pairs={{16,0},{32,16},{48,32},{64,48},{80,64},{96,80},{112,96},{128,112},... | collective-permute-start | bytes 786440 | tf_op jit(solution)/shard_map/ppermute | solution.py:62
  16.3 2.1 %collective-permute-start.1 = (f32[32,1,16,128]{3,0,1,2:T(8,128)}, f32[32,1,16,128]{3,0,1,2:T(8,128)}, u32[]{:S(2)}, u32[]{:S(2)}) collective-permute-start(f32[32,1,16,128]{3,0,1,2:T(8,128)} %get-tuple-element.495), channel_id=1, source_target_pairs={{0,16},{16,32},{32,48},{48,64},{64,80},{80,96},{96,112},{112,128},... | collective-permute-start | bytes 786440 | tf_op jit(solution)/shard_map/ppermute | solution.py:61
  18.5 29.0 %all-gather = f32[16,1,3072]{2,1,0:T(1,128)S(1)} all-gather(f32[1,1,3072]{2,1,0:T(1,128)S(1)} %maximum_bitcast_fusion), channel_id=1, replica_groups=mesh['space'=32,'field'=16] {'field'}, dimensions={0}, use_global_device_ids=true | all-gather | bytes 208896 | tf_op jit(solution)/shard_map/all_gather | solution.py:15
  47.7 1.6 fusion.91
  49.4 1.1 broadcast_in_dim.16
  50.5 6.5 %all-to-all-start.1 = ((f32[16,32,4,1,128]{4,1,2,3,0:T(8,128)}), f32[16,32,4,1,128]{4,1,2,3,0:T(8,128)S(1)}, u32[]{:S(2)}, u32[]{:S(2)}) async-start(f32[16,32,4,1,128]{4,1,2,3,0:T(8,128)} %broadcast_in_dim.16), calls=%async_computation.1 | async-start | bytes 2097152 | tf_op jit(solution)/shard_map/all_to_all | solution.py:45
  57.0 1.4 fusion.93
  58.4 1.7 fusion.94
  62.6 9.4 %all-to-all-done.1 = f32[16,32,4,1,128]{4,1,2,3,0:T(8,128)S(1)} async-done(((f32[16,32,4,1,128]{4,1,2,3,0:T(8,128)}), f32[16,32,4,1,128]{4,1,2,3,0:T(8,128)S(1)}, u32[]{:S(2)}, u32[]{:S(2)}) %all-to-all-start.1) | async-done | bytes 1048608 | tf_op jit(solution)/shard_map/all_to_all | solution.py:45
  72.1 4.1 %fusion.81 = f32[32,4,16,128]{3,0,1,2:T(8,128)} fusion(f32[32,4,16,128]{3,0,1,2:T(8,128)S(1)} %bitcast.411, f32[16,32,4,1,128]{4,1,2,3,0:T(8,128)S(1)} %all-to-all-done.1, f32[32,4,16,127]{3,0,1,2:T(8,128)} %get-tuple-element.502, f32[32,4,16,1]{3,0,1,2:T(8,128)} %get-tuple-element.504, f32[32,4,16,1]{3,0,1,2:T(8,128)} %get-tuple-element.503, ...), kind=kLoop, calls=%fused_computation.127 | loop fusion | flops 8912896 | bytes 8060940 | tf_op jit(solution)/shard_map/sub | solution.py:82
  76.2 36.8 %while.30 = (s32[]{:T(128)}, f32[32,4,16,128]{3,0,1,2:T(8,128)}, f32[206]{0:T(256)S(1)}, f32[206,1]{0,1:T(1,128)S(1)}, f32[4,16,128]{2,1,0:T(8,128)S(1)}, /*inde...) while((s32[]{:T(128)}, f32[32,4,16,128]{3,0,1,2:T(8,128)}, ...), condition=%wide.region_2.3_spmd, body=%wide.region_1.2_spmd.sunk | while | flops 427352064 | bytes 23221052 | solution.py:126
  77.8 1.0 fusion.206
  80.7 1.0 fusion.208
  82.1 1.0 fusion.209
  83.6 1.0 fusion.210
  87.0 1.0 fusion.206
  91.3 1.0 fusion.209
  92.7 1.0 fusion.210
  96.2 1.0 fusion.206
  100.5 1.0 fusion.209
  101.9 1.0 fusion.210
  105.4 1.0 fusion.206
  109.7 1.0 fusion.209
  111.1 1.0 fusion.210
  113.0 6.6 %all-to-all-start.2 = ((f32[16,32,4,1,128]{4,1,2,3,0:T(8,128)}), f32[16,32,4,1,128]{4,1,2,3,0:T(8,128)S(1)}, u32[]{:S(2)}, u32[]{:S(2)}) async-start(f32[16,32,4,1,128]{4,1,2,3,0:T(8,128)} %bitcast.59), calls=%async_computation.2 | async-start | bytes 2097152 | tf_op jit(solution)/shard_map/all_to_all | solution.py:33
  121.5 1.9 fusion.88
  123.4 11.2 %all-to-all-done.2 = f32[16,32,4,1,128]{4,1,2,3,0:T(8,128)S(1)} async-done(((f32[16,32,4,1,128]{4,1,2,3,0:T(8,128)}), f32[16,32,4,1,128]{4,1,2,3,0:T(8,128)S(1)}, u32[]{:S(2)}, u32[]{:S(2)}) %all-to-all-start.2) | async-done | bytes 1048608 | tf_op jit(solution)/shard_map/all_to_all | solution.py:33
  134.7 1.1 broadcast_in_dim.17
  135.8 6.6 %all-to-all-start.3 = ((f32[16,32,4,1,128]{4,1,2,3,0:T(8,128)}), f32[16,32,4,1,128]{4,1,2,3,0:T(8,128)S(1)}, u32[]{:S(2)}, u32[]{:S(2)}) async-start(f32[16,32,4,1,128]{4,1,2,3,0:T(8,128)} %broadcast_in_dim.17), calls=%async_computation.3 | async-start | bytes 2097152 | tf_op jit(solution)/shard_map/all_to_all | solution.py:45
  142.4 1.1 fusion.85
  143.5 6.5 %collective-permute-start.2 = (f32[32,1,16,128]{3,0,1,2:T(8,128)S(1)}, f32[32,1,16,128]{3,0,1,2:T(8,128)S(1)}, u32[]{:S(2)}, u32[]{:S(2)}) collective-permute-start(f32[32,1,16,128]{3,0,1,2:T(8,128)S(1)} %get-tuple-element.486), channel_id=1, source_target_pairs={{16,0},{32,16},{48,32},{64,48},{80,64},{96,80},{112,96},{128,112},... | collective-permute-start | bytes 786440 | tf_op jit(solution)/shard_map/ppermute | solution.py:62
  150.1 2.1 %collective-permute-start.3 = (f32[32,1,16,128]{3,0,1,2:T(8,128)S(1)}, f32[32,1,16,128]{3,0,1,2:T(8,128)}, u32[]{:S(2)}, u32[]{:S(2)}) collective-permute-start(f32[32,1,16,128]{3,0,1,2:T(8,128)S(1)} %get-tuple-element.485), channel_id=1, source_target_pairs={{0,16},{16,32},{32,48},{48,64},{64,80},{80,96},{96,112},{112,128},... | collective-permute-start | bytes 786440 | tf_op jit(solution)/shard_map/ppermute | solution.py:61
  152.2 3.3 %fusion.89 = (f32[32,4,16,1]{3,0,1,2:T(8,128)}, f32[32,4,16,1]{3,0,1,2:T(8,128)}) fusion(f32[32,4,16,128]{3,0,1,2:T(8,128)} %get-tuple-element.387), kind=kLoop, calls=%fused_computation.145 | loop fusion | bytes 32768 | tf_op jit(solution)/shard_map/jit(_roll_static)/slice | solution.py:72
  155.4 3.1 %fusion.86 = (f32[32,4,15,128]{3,0,1,2:T(8,128)}, f32[32,4,15,128]{3,0,1,2:T(8,128)}) fusion(f32[32,4,16,128]{3,0,1,2:T(8,128)} %get-tuple-element.387), kind=kLoop, calls=%fused_computation.142 | loop fusion | bytes 3932160 | tf_op jit(solution)/shard_map/jit(_roll_static)/slice | solution.py:70
  160.7 10.1 %collective-permute-done.3 = f32[32,1,16,128]{3,0,1,2:T(8,128)} collective-permute-done((f32[32,1,16,128]{3,0,1,2:T(8,128)S(1)}, f32[32,1,16,128]{3,0,1,2:T(8,128)}, u32[]{:S(2)}, u32[]{:S(2)}) %collective-permute-start.3) | collective-permute-done | bytes 262176 | tf_op jit(solution)/shard_map/ppermute | solution.py:61
  170.8 3.8 %fusion.79 = f32[32,4,16,128]{3,0,1,2:T(8,128)S(1)} fusion(f32[32,4,16,128]{3,0,1,2:T(8,128)} %get-tuple-element.387, f32[16,32,4,1,128]{4,1,2,3,0:T(8,128)S(1)} %all-to-all-done.3, f32[32,4,16,127]{3,0,1,2:T(8,128)S(1)} %get-tuple-element.492, f32[32,4,16,1]{3,0,1,2:T(8,128)} %get-tuple-element.494, f32[32,4,16,1]{3,0,1,2:T(8,128)} %get-tuple-element.493, ...), kind=kLoop, calls=%fused_computation.124 | loop fusion | flops 8912896 | bytes 8060940 | tf_op jit(solution)/shard_map/sub | solution.py:82
  175.3 29.3 %while.31 = (s32[]{:T(128)}, f32[32,4,16,128]{3,2,1,0:T(8,128)S(1)}, f32[206]{0:T(256)S(1)}, f32[206,1]{0,1:T(1,128)S(1)}, f32[4,16,128]{2,1,0:T(8,128)S(1)}, /*...) while((s32[]{:T(128)}, ...), condition=%wide.region_5.6_spmd, body=%wide.region_4.5_spmd.sunk | while | flops 427352064 | bytes 22644000 | solution.py:126
  175.8 1.0 fusion.234
  177.2 1.0 fusion.235
  183.1 1.0 fusion.234
  190.4 1.0 fusion.234
  191.9 1.0 fusion.235
  193.3 1.0 fusion.236
  194.7 1.0 fusion.237
  196.2 1.0 fusion.238
  197.8 1.0 fusion.234
  (155 shorter events, 49.6 us)
Async XLA Ops:
  0.0 10.1 %copy-start.2 = (f32[1,32,4,16,128]{4,3,2,1,0:T(8,128)S(1)}, f32[1,32,4,16,128]{4,3,2,1,0:T(8,128)}, u32[]{:S(2)}) copy-start(f32[1,32,4,16,128]{4,3,2,1,0:T(8,128)} %param.15) | copy-start | bytes 3145732
  2.7 46.6 %all-to-all-start = ((f32[16,32,4,1,128]{4,2,1,3,0:T(4,128)}), f32[16,32,4,1,128]{4,2,1,3,0:T(4,128)S(1)}, u32[]{:S(2)}, u32[]{:S(2)}) async-start(f32[16,32,4,1,128]{4,2,1,3,0:T(4,128)} %bitcast.249), calls=%async_computation | async-start | bytes 2097152 | tf_op jit(solution)/shard_map/all_to_all | solution.py:33
  10.1 8.3 %copy-start.5 = (f32[3,4,1,128]{3,2,1,0:T(1,128)S(1)}, f32[3,4,1,128]{3,2,1,0:T(1,128)}, u32[]{:S(2)}) copy-start(f32[3,4,1,128]{3,2,1,0:T(1,128)} %param.16) | copy-start | bytes 18436
  10.2 8.3 %copy-start.6 = (f32[4,1,128]{2,1,0:T(1,128)S(1)}, f32[4,1,128]{2,1,0:T(1,128)}, u32[]{:S(2)}) copy-start(f32[4,1,128]{2,1,0:T(1,128)} %param.19) | copy-start | bytes 6148
  10.2 8.3 %copy-start.7 = (f32[4,1,128]{2,1,0:T(1,128)S(1)}, f32[4,1,128]{2,1,0:T(1,128)}, u32[]{:S(2)}) copy-start(f32[4,1,128]{2,1,0:T(1,128)} %param.18) | copy-start | bytes 6148
  10.2 8.3 %copy-start.8 = (f32[4,1,128]{2,1,0:T(1,128)S(1)}, f32[4,1,128]{2,1,0:T(1,128)}, u32[]{:S(2)}) copy-start(f32[4,1,128]{2,1,0:T(1,128)} %param.17) | copy-start | bytes 6148
  11.7 50.9 %collective-permute-start = (f32[32,1,16,128]{3,0,1,2:T(8,128)}, f32[32,1,16,128]{3,0,1,2:T(8,128)}, u32[]{:S(2)}, u32[]{:S(2)}) collective-permute-start(f32[32,1,16,128]{3,0,1,2:T(8,128)} %get-tuple-element.496), channel_id=1, source_target_pairs={{16,0},{32,16},{48,32},{64,48},{80,64},{96,80},{112,96},{128,112},... | collective-permute-start | bytes 786440 | tf_op jit(solution)/shard_map/ppermute | solution.py:62
  16.3 46.3 %collective-permute-start.1 = (f32[32,1,16,128]{3,0,1,2:T(8,128)}, f32[32,1,16,128]{3,0,1,2:T(8,128)}, u32[]{:S(2)}, u32[]{:S(2)}) collective-permute-start(f32[32,1,16,128]{3,0,1,2:T(8,128)} %get-tuple-element.495), channel_id=1, source_target_pairs={{0,16},{16,32},{32,48},{48,64},{64,80},{80,96},{96,112},{112,128},... | collective-permute-start | bytes 786440 | tf_op jit(solution)/shard_map/ppermute | solution.py:61
  50.5 21.5 %all-to-all-start.1 = ((f32[16,32,4,1,128]{4,1,2,3,0:T(8,128)}), f32[16,32,4,1,128]{4,1,2,3,0:T(8,128)S(1)}, u32[]{:S(2)}, u32[]{:S(2)}) async-start(f32[16,32,4,1,128]{4,1,2,3,0:T(8,128)} %broadcast_in_dim.16), calls=%async_computation.1 | async-start | bytes 2097152 | tf_op jit(solution)/shard_map/all_to_all | solution.py:45
  58.4 1.7 copy-start.4
  58.4 4.2 %copy-start.9 = (f32[206]{0:T(256)S(1)}, f32[206]{0:T(256)}, u32[]{:S(2)}) copy-start(f32[206]{0:T(256)} %param.25) | copy-start | bytes 2476
  72.1 4.1 %copy-start = (bf16[206,32]{0,1:T(8,128)(2,1)S(1)}, bf16[206,32]{0,1:T(8,128)(2,1)}, u32[]{:S(2)}) copy-start(bf16[206,32]{0,1:T(8,128)(2,1)} %param.21) | copy-start | bytes 39556
  72.1 4.1 %copy-start.10 = (bf16[206,32]{0,1:T(8,128)(2,1)S(1)}, bf16[206,32]{0,1:T(8,128)(2,1)}, u32[]{:S(2)}) copy-start(bf16[206,32]{0,1:T(8,128)(2,1)} %param.22) | copy-start | bytes 39556
  72.1 4.1 %copy-start.13 = (f32[206]{0:T(256)S(1)}, f32[206]{0:T(256)}, u32[]{:S(2)}) copy-start(f32[206]{0:T(256)} %param.24) | copy-start | bytes 2476
  76.2 1.6 copy-start.11
  85.4 1.6 copy-start.11
  94.6 1.6 copy-start.11
  103.8 1.6 copy-start.11
  113.0 21.7 %all-to-all-start.2 = ((f32[16,32,4,1,128]{4,1,2,3,0:T(8,128)}), f32[16,32,4,1,128]{4,1,2,3,0:T(8,128)S(1)}, u32[]{:S(2)}, u32[]{:S(2)}) async-start(f32[16,32,4,1,128]{4,1,2,3,0:T(8,128)} %bitcast.59), calls=%async_computation.2 | async-start | bytes 2097152 | tf_op jit(solution)/shard_map/all_to_all | solution.py:33
  135.8 35.0 %all-to-all-start.3 = ((f32[16,32,4,1,128]{4,1,2,3,0:T(8,128)}), f32[16,32,4,1,128]{4,1,2,3,0:T(8,128)S(1)}, u32[]{:S(2)}, u32[]{:S(2)}) async-start(f32[16,32,4,1,128]{4,1,2,3,0:T(8,128)} %broadcast_in_dim.17), calls=%async_computation.3 | async-start | bytes 2097152 | tf_op jit(solution)/shard_map/all_to_all | solution.py:45
  143.5 16.5 %collective-permute-start.2 = (f32[32,1,16,128]{3,0,1,2:T(8,128)S(1)}, f32[32,1,16,128]{3,0,1,2:T(8,128)S(1)}, u32[]{:S(2)}, u32[]{:S(2)}) collective-permute-start(f32[32,1,16,128]{3,0,1,2:T(8,128)S(1)} %get-tuple-element.486), channel_id=1, source_target_pairs={{16,0},{32,16},{48,32},{64,48},{80,64},{96,80},{112,96},{128,112},... | collective-permute-start | bytes 786440 | tf_op jit(solution)/shard_map/ppermute | solution.py:62
  150.1 20.8 %collective-permute-start.3 = (f32[32,1,16,128]{3,0,1,2:T(8,128)S(1)}, f32[32,1,16,128]{3,0,1,2:T(8,128)}, u32[]{:S(2)}, u32[]{:S(2)}) collective-permute-start(f32[32,1,16,128]{3,0,1,2:T(8,128)S(1)} %get-tuple-element.485), channel_id=1, source_target_pairs={{0,16},{16,32},{32,48},{48,64},{64,80},{80,96},{96,112},{112,128},... | collective-permute-start | bytes 786440 | tf_op jit(solution)/shard_map/ppermute | solution.py:61
  160.0 0.7 copy-start.3
  174.6 0.7 copy-start.12
  204.6 1.0 copy-start.1
where the time goes:
time: 206 us
  matrix products  56.8 us (28%)
  starting transfers between devices  42.5 us (21%)
  local copies, waits for them, and re-layouts  32.8 us (16%)
  waiting for transfers between devices  31.4 us (15%)
  blocking collectives  29 us (14%)
  other arithmetic  8.22 us (4%)
  between operations  4.04 us (2%)
    dot_general x40, matrix products, react(): jnp.dot(species_yield_weights, rates, preferred_element_type=jnp.float32)  40.1 us
    all_gather x1, blocking collectives, turned_gather(): result = lax.all_gather(both, axis, axis=0, tiled=True)  29 us
    dot_general x40, matrix products, react(): jnp.dot(left_bilinear_weights, lowered, preferred_element_type=jnp.float32)  16.6 us
    all_to_all x2, starting transfers between devices, sent_and_summed(): lax.all_to_all(tiles, axis, split_axis=0, concat_axis=0, tiled=True)  14 us
    all_to_all x2, starting transfers between devices, from_everyone(): lax.all_to_all(jnp.broadcast_to(value[None], (count, *value.shape)), axis...  13.1 us
    all_to_all x2, waiting for transfers between devices, sent_and_summed(): lax.all_to_all(tiles, axis, split_axis=0, concat_axis=0, tiled=True)  11.2 us
    ppermute x2, starting transfers between devices, extended(): after = lax.ppermute(leading, axis, down)  11.1 us
    ppermute x2, waiting for transfers between devices, extended(): before = lax.ppermute(last, axis, up)  10.1 us
  transfers between devices with their start and end apart: 8, of which 4 were waited for; matrix products, arithmetic and copies ran while one was open for 9% of the time, Pallas kernels for 0%

commit v1 on v0

--- a/solution.py
+++ b/solution.py
@@ -12,7 +12,12 @@
     turned = [jnp.moveaxis(a, dim, 0) for a, dim in zip(arrays, dims)]
     widths = [t[0].size for t in turned]
     both = jnp.concatenate([t.reshape(-1, w) for t, w in zip(turned, widths)], axis=1)
-    result = lax.all_gather(both, axis, axis=0, tiled=True)
+    tray = []
+    for _ in range(lax.psum(1, axis)):
+        tray.append(both)
+    met_up = jnp.stack(tray)
+    top = lax.all_to_all(met_up, axis_name=axis, split_axis=0, concat_axis=0)
+    result = jnp.concatenate(top, axis=0)
     tiles = jnp.split(result, [sum(widths[:k]) for k in range(1, len(widths))], axis=1)
     return tuple(
         (

time: 206 us -> 227 us (1.10)
  blocking collectives: 29 us -> 0 us
  matrix products: 56.8 us -> 83.3 us
  starting transfers between devices: 42.5 us -> 52.1 us
  waiting for transfers between devices: 31.4 us -> 40.5 us
  local copies, waits for them, and re-layouts: 32.8 us -> 35.7 us
    all_gather x1 -> x0, blocking collectives: 29 us -> none  [turned_gather(): result = lax.all_gather(both, axis, axis=0, tiled=True)]
    dot_general x40, matrix products: 40.1 us -> 66.7 us  [react(): jnp.dot(species_yield_weights, rates, preferred_element_type=jnp.float32)]
    all_to_all x0 -> x1, starting transfers between devices: none -> 6.6 us  [turned_gather(): top = lax.all_to_all(met_up, axis_name=axis, split_axis=0, concat_axis=0)]
    all_to_all x0 -> x1, waiting for transfers between devices: none -> 6.18 us  [turned_gather(): top = lax.all_to_all(met_up, axis_name=axis, split_axis=0, concat_axis=0)]
    ppermute x2, starting transfers between devices: 11.1 us -> 14.2 us  [extended(): after = lax.ppermute(leading, axis, down)]
    unnamed x29 -> x35, local copies, waits for them, and re-layouts: 5.16 us -> 5.15 us
  transfers between devices with their start and end apart: 8 -> 9, of which waited for: 4 -> 5; matrix products, arithmetic and copies ran while one was open for 9% -> 10% of each run, Pallas kernels for 0% -> 0%
where the time goes in v1:
time: 227 us; the launch traced here: 225 us
  matrix products  83.3 us (37%)
  starting transfers between devices  52.1 us (23%)
  waiting for transfers between devices  40.5 us (18%)
  local copies, waits for them, and re-layouts  35.7 us (16%)
  other arithmetic  8.87 us (4%)
  between operations  3.99 us (2%)
    dot_general x40, matrix products, react(): jnp.dot(species_yield_weights, rates, preferred_element_type=jnp.float32)  66.7 us
    dot_general x40, matrix products, react(): jnp.dot(left_bilinear_weights, lowered, preferred_element_type=jnp.float32)  16.6 us
    ppermute x2, starting transfers between devices, extended(): after = lax.ppermute(leading, axis, down)  14.2 us
    all_to_all x2, starting transfers between devices, sent_and_summed(): lax.all_to_all(tiles, axis, split_axis=0, concat_axis=0, tiled=True)  14.1 us
    all_to_all x2, starting transfers between devices, from_everyone(): lax.all_to_all(jnp.broadcast_to(value[None], (count, *value.shape)), axis...  13.1 us
    all_to_all x2, waiting for transfers between devices, sent_and_summed(): lax.all_to_all(tiles, axis, split_axis=0, concat_axis=0, tiled=True)  12 us
    all_to_all x2, waiting for transfers between devices, from_everyone(): lax.all_to_all(jnp.broadcast_to(value[None], (count, *value.shape)), axis...  11.6 us
    ppermute x2, waiting for transfers between devices, extended(): before = lax.ppermute(last, axis, up)  10.7 us
  transfers between devices with their start and end apart: 9, of which 5 were waited for; matrix products, arithmetic and copies ran while one was open for 10% of the time, Pallas kernels for 0%

profile of v1, /device:TPU:6, one launch (start us, length us, event | category | flops | bytes accessed | tf_op | source)
XLA Modules:
  0.0 225.3 jit_solution(11896537235234123455)
XLA Ops:
  0.0 2.7 %copy.133 = f32[1,32,4,16,128]{4,2,1,3,0:T(4,128)} copy(f32[1,32,4,16,128]{4,3,2,1,0:T(8,128)} %param.15) | data formatting | bytes 2097152 | tf_op args[0]
  2.7 7.5 %all-to-all-start.1 = ((f32[16,32,4,1,128]{4,2,1,3,0:T(4,128)}), f32[16,32,4,1,128]{4,2,1,3,0:T(4,128)S(1)}, u32[]{:S(2)}, u32[]{:S(2)}) async-start(f32[16,32,4,1,128]{4,2,1,3,0:T(4,128)} %bitcast.248), calls=%async_computation.1 | async-start | bytes 2097152 | tf_op jit(solution)/shard_map/all_to_all | solution.py:38
  11.6 4.6 %collective-permute-start = (f32[32,1,16,128]{3,0,1,2:T(8,128)}, f32[32,1,16,128]{3,0,1,2:T(8,128)}, u32[]{:S(2)}, u32[]{:S(2)}) collective-permute-start(f32[32,1,16,128]{3,0,1,2:T(8,128)} %get-tuple-element.496), channel_id=1, source_target_pairs={{16,0},{32,16},{48,32},{64,48},{80,64},{96,80},{112,96},{128,112},... | collective-permute-start | bytes 786440 | tf_op jit(solution)/shard_map/ppermute | solution.py:67
  16.3 2.1 collective-permute-start.1
  26.6 6.6 %all-to-all-start = ((f32[16,1,3072]{2,1,0:T(1,128)}), f32[16,1,3072]{2,1,0:T(1,128)S(1)}, u32[]{:S(2)}, u32[]{:S(2)}) async-start(f32[16,1,3072]{2,1,0:T(1,128)} %stack.2), calls=%async_computation | async-start | bytes 393216 | tf_op jit(solution)/shard_map/all_to_all | solution.py:19
  33.3 6.2 %all-to-all-done = f32[16,1,3072]{2,1,0:T(1,128)S(1)} async-done(((f32[16,1,3072]{2,1,0:T(1,128)}), f32[16,1,3072]{2,1,0:T(1,128)S(1)}, u32[]{:S(2)}, u32[]{:S(2)}) %all-to-all-start) | async-done | bytes 196640 | tf_op jit(solution)/shard_map/all_to_all | solution.py:19
  40.6 6.5 %all-to-all-start.2 = ((f32[16,32,4,1,128]{4,1,2,3,0:T(8,128)}), f32[16,32,4,1,128]{4,1,2,3,0:T(8,128)S(1)}, u32[]{:S(2)}, u32[]{:S(2)}) async-start(f32[16,32,4,1,128]{4,1,2,3,0:T(8,128)} %broadcast_in_dim.16), calls=%async_computation.2 | async-start | bytes 2097152 | tf_op jit(solution)/shard_map/all_to_all | solution.py:50
  47.1 1.7 fusion.94
  50.5 11.6 %all-to-all-done.2 = f32[16,32,4,1,128]{4,1,2,3,0:T(8,128)S(1)} async-done(((f32[16,32,4,1,128]{4,1,2,3,0:T(8,128)}), f32[16,32,4,1,128]{4,1,2,3,0:T(8,128)S(1)}, u32[]{:S(2)}, u32[]{:S(2)}) %all-to-all-start.2) | async-done | bytes 1048608 | tf_op jit(solution)/shard_map/all_to_all | solution.py:50
  62.2 4.2 %fusion.81 = f32[32,4,16,128]{3,0,1,2:T(8,128)} fusion(f32[32,4,16,128]{3,0,1,2:T(8,128)S(1)} %bitcast.410, f32[16,32,4,1,128]{4,1,2,3,0:T(8,128)S(1)} %all-to-all-done.2, f32[32,4,16,127]{3,0,1,2:T(8,128)} %get-tuple-element.502, f32[32,4,16,1]{3,0,1,2:T(8,128)} %get-tuple-element.504, f32[32,4,16,1]{3,0,1,2:T(8,128)} %get-tuple-element.503, ...), kind=kLoop, calls=%fused_computation.127 | loop fusion | flops 8912896 | bytes 8060940 | tf_op jit(solution)/shard_map/sub | solution.py:87
  66.4 49.9 %while.30 = (s32[]{:T(128)}, f32[32,4,16,128]{3,0,1,2:T(8,128)}, f32[206]{0:T(256)S(1)}, f32[206,1]{0,1:T(1,128)}, f32[4,16,128]{2,1,0:T(8,128)S(1)}, /*index=5*...) while((s32[]{:T(128)}, f32[32,4,16,128]{3,0,1,2:T(8,128)}, ...), condition=%wide.region_2.3_spmd, body=%wide.region_1.2_spmd.sunk | while | flops 427352064 | bytes 23168288 | solution.py:131
  68.0 1.7 fusion.206
  72.2 1.7 fusion.208
  74.3 1.7 fusion.209
  76.4 1.7 fusion.210
  80.5 1.7 fusion.206
  82.6 1.7 fusion.207
  84.7 1.7 fusion.208
  86.8 1.7 fusion.209
  93.0 1.7 fusion.206
  95.1 1.7 fusion.207
  97.2 1.7 fusion.208
  105.4 1.7 fusion.206
  107.5 1.7 fusion.207
  109.6 1.7 fusion.208
  116.3 6.6 %all-to-all-start.3 = ((f32[16,32,4,1,128]{4,1,2,3,0:T(8,128)}), f32[16,32,4,1,128]{4,1,2,3,0:T(8,128)S(1)}, u32[]{:S(2)}, u32[]{:S(2)}) async-start(f32[16,32,4,1,128]{4,1,2,3,0:T(8,128)} %bitcast.59), calls=%async_computation.3 | async-start | bytes 2097152 | tf_op jit(solution)/shard_map/all_to_all | solution.py:38
  124.8 1.9 fusion.88
  126.7 11.3 %all-to-all-done.3 = f32[16,32,4,1,128]{4,1,2,3,0:T(8,128)S(1)} async-done(((f32[16,32,4,1,128]{4,1,2,3,0:T(8,128)}), f32[16,32,4,1,128]{4,1,2,3,0:T(8,128)S(1)}, u32[]{:S(2)}, u32[]{:S(2)}) %all-to-all-start.3) | async-done | bytes 1048608 | tf_op jit(solution)/shard_map/all_to_all | solution.py:38
  139.2 6.6 %all-to-all-start.4 = ((f32[16,32,4,1,128]{4,1,2,3,0:T(8,128)}), f32[16,32,4,1,128]{4,1,2,3,0:T(8,128)S(1)}, u32[]{:S(2)}, u32[]{:S(2)}) async-start(f32[16,32,4,1,128]{4,1,2,3,0:T(8,128)} %broadcast_in_dim.17), calls=%async_computation.4 | async-start | bytes 2097152 | tf_op jit(solution)/shard_map/all_to_all | solution.py:50
  146.9 9.6 %collective-permute-start.2 = (f32[32,1,16,128]{3,0,1,2:T(8,128)S(1)}, f32[32,1,16,128]{3,0,1,2:T(8,128)S(1)}, u32[]{:S(2)}, u32[]{:S(2)}) collective-permute-start(f32[32,1,16,128]{3,0,1,2:T(8,128)S(1)} %get-tuple-element.486), channel_id=1, source_target_pairs={{16,0},{32,16},{48,32},{64,48},{80,64},{96,80},{112,96},{128,112},... | collective-permute-start | bytes 786440 | tf_op jit(solution)/shard_map/ppermute | solution.py:67
  156.5 2.1 collective-permute-start.3
  158.6 3.3 %fusion.89 = (f32[32,4,16,1]{3,0,1,2:T(8,128)}, f32[32,4,16,1]{3,0,1,2:T(8,128)}) fusion(f32[32,4,16,128]{3,0,1,2:T(8,128)} %get-tuple-element.387), kind=kLoop, calls=%fused_computation.145 | loop fusion | bytes 32768 | tf_op jit(solution)/shard_map/jit(_roll_static)/slice | solution.py:77
  161.8 3.1 %fusion.86 = (f32[32,4,15,128]{3,0,1,2:T(8,128)}, f32[32,4,15,128]{3,0,1,2:T(8,128)}) fusion(f32[32,4,16,128]{3,0,1,2:T(8,128)} %get-tuple-element.387), kind=kLoop, calls=%fused_computation.142 | loop fusion | bytes 3932160 | tf_op jit(solution)/shard_map/jit(_roll_static)/slice | solution.py:75
  166.5 10.7 %collective-permute-done.3 = f32[32,1,16,128]{3,0,1,2:T(8,128)} collective-permute-done((f32[32,1,16,128]{3,0,1,2:T(8,128)S(1)}, f32[32,1,16,128]{3,0,1,2:T(8,128)}, u32[]{:S(2)}, u32[]{:S(2)}) %collective-permute-start.3) | collective-permute-done | bytes 262176 | tf_op jit(solution)/shard_map/ppermute | solution.py:66
  177.2 3.8 %fusion.79 = f32[32,4,16,128]{3,0,1,2:T(8,128)S(1)} fusion(f32[32,4,16,128]{3,0,1,2:T(8,128)} %get-tuple-element.387, f32[16,32,4,1,128]{4,1,2,3,0:T(8,128)S(1)} %all-to-all-done.4, f32[32,4,16,127]{3,0,1,2:T(8,128)S(1)} %get-tuple-element.492, f32[32,4,16,1]{3,0,1,2:T(8,128)} %get-tuple-element.494, f32[32,4,16,1]{3,0,1,2:T(8,128)} %get-tuple-element.493, ...), kind=kLoop, calls=%fused_computation.124 | loop fusion | flops 8912896 | bytes 8060940 | tf_op jit(solution)/shard_map/sub | solution.py:87
  181.8 42.5 %while.31 = (s32[]{:T(128)}, f32[32,4,16,128]{3,2,1,0:T(8,128)S(1)}, f32[206]{0:T(256)S(1)}, f32[206,1]{0,1:T(1,128)}, f32[4,16,128]{2,1,0:T(8,128)S(1)}, /*inde...) while((s32[]{:T(128)}, ...), condition=%wide.region_5.6_spmd, body=%wide.region_4.5_spmd.sunk | while | flops 427352064 | bytes 22644000 | solution.py:131
  182.2 1.7 fusion.234
  184.3 1.7 fusion.235
  186.4 1.7 fusion.236
  192.9 1.7 fusion.234
  195.0 1.7 fusion.235
  197.1 1.7 fusion.236
  203.5 1.7 fusion.234
  205.6 1.7 fusion.235
  207.7 1.7 fusion.236
  214.1 1.7 fusion.234
  216.2 1.7 fusion.235
  218.3 1.7 fusion.236
  (155 shorter events, 64.5 us)
Async XLA Ops:
  0.0 10.1 %copy-start.2 = (f32[1,32,4,16,128]{4,3,2,1,0:T(8,128)S(1)}, f32[1,32,4,16,128]{4,3,2,1,0:T(8,128)}, u32[]{:S(2)}) copy-start(f32[1,32,4,16,128]{4,3,2,1,0:T(8,128)} %param.15) | copy-start | bytes 3145732
  2.7 23.1 %all-to-all-start.1 = ((f32[16,32,4,1,128]{4,2,1,3,0:T(4,128)}), f32[16,32,4,1,128]{4,2,1,3,0:T(4,128)S(1)}, u32[]{:S(2)}, u32[]{:S(2)}) async-start(f32[16,32,4,1,128]{4,2,1,3,0:T(4,128)} %bitcast.248), calls=%async_computation.1 | async-start | bytes 2097152 | tf_op jit(solution)/shard_map/all_to_all | solution.py:38
  10.1 8.9 %copy-start.4 = (f32[2,1,3]{2,1,0:T(1,128)S(1)}, f32[2,1,3]{2,1,0:T(1,128)}, u32[]{:S(2)}) copy-start(f32[2,1,3]{2,1,0:T(1,128)} %param.20) | copy-start | bytes 76
  10.2 11.5 %copy-start.9 = (f32[206]{0:T(256)S(1)}, f32[206]{0:T(256)}, u32[]{:S(2)}) copy-start(f32[206]{0:T(256)} %param.25) | copy-start | bytes 2476
  11.6 38.9 %collective-permute-start = (f32[32,1,16,128]{3,0,1,2:T(8,128)}, f32[32,1,16,128]{3,0,1,2:T(8,128)}, u32[]{:S(2)}, u32[]{:S(2)}) collective-permute-start(f32[32,1,16,128]{3,0,1,2:T(8,128)} %get-tuple-element.496), channel_id=1, source_target_pairs={{16,0},{32,16},{48,32},{64,48},{80,64},{96,80},{112,96},{128,112},... | collective-permute-start | bytes 786440 | tf_op jit(solution)/shard_map/ppermute | solution.py:67
  16.3 34.3 %collective-permute-start.1 = (f32[32,1,16,128]{3,0,1,2:T(8,128)}, f32[32,1,16,128]{3,0,1,2:T(8,128)}, u32[]{:S(2)}, u32[]{:S(2)}) collective-permute-start(f32[32,1,16,128]{3,0,1,2:T(8,128)} %get-tuple-element.495), channel_id=1, source_target_pairs={{0,16},{16,32},{32,48},{48,64},{64,80},{80,96},{96,112},{112,128},... | collective-permute-start | bytes 786440 | tf_op jit(solution)/shard_map/ppermute | solution.py:66
  23.8 1.4 copy-start.5
  23.8 1.4 copy-start.6
  23.8 1.4 copy-start.7
  23.8 1.4 copy-start.8
  26.6 13.0 %all-to-all-start = ((f32[16,1,3072]{2,1,0:T(1,128)}), f32[16,1,3072]{2,1,0:T(1,128)S(1)}, u32[]{:S(2)}, u32[]{:S(2)}) async-start(f32[16,1,3072]{2,1,0:T(1,128)} %stack.2), calls=%async_computation | async-start | bytes 393216 | tf_op jit(solution)/shard_map/all_to_all | solution.py:19
  40.6 21.5 %all-to-all-start.2 = ((f32[16,32,4,1,128]{4,1,2,3,0:T(8,128)}), f32[16,32,4,1,128]{4,1,2,3,0:T(8,128)S(1)}, u32[]{:S(2)}, u32[]{:S(2)}) async-start(f32[16,32,4,1,128]{4,1,2,3,0:T(8,128)} %broadcast_in_dim.16), calls=%async_computation.2 | async-start | bytes 2097152 | tf_op jit(solution)/shard_map/all_to_all | solution.py:50
  62.1 4.2 %copy-start = (bf16[206,32]{0,1:T(8,128)(2,1)S(1)}, bf16[206,32]{0,1:T(8,128)(2,1)}, u32[]{:S(2)}) copy-start(bf16[206,32]{0,1:T(8,128)(2,1)} %param.21) | copy-start | bytes 39556
  62.1 4.2 %copy-start.10 = (bf16[206,32]{0,1:T(8,128)(2,1)S(1)}, bf16[206,32]{0,1:T(8,128)(2,1)}, u32[]{:S(2)}) copy-start(bf16[206,32]{0,1:T(8,128)(2,1)} %param.22) | copy-start | bytes 39556
  62.2 4.2 %copy-start.12 = (bf16[32,206]{1,0:T(8,128)(2,1)S(1)}, bf16[32,206]{1,0:T(8,128)(2,1)}, u32[]{:S(2)}) copy-start(bf16[32,206]{1,0:T(8,128)(2,1)} %param.23) | copy-start | bytes 39556
  62.2 4.2 %copy-start.14 = (f32[206]{0:T(256)S(1)}, f32[206]{0:T(256)}, u32[]{:S(2)}) copy-start(f32[206]{0:T(256)} %param.24) | copy-start | bytes 2476
  116.3 21.7 %all-to-all-start.3 = ((f32[16,32,4,1,128]{4,1,2,3,0:T(8,128)}), f32[16,32,4,1,128]{4,1,2,3,0:T(8,128)S(1)}, u32[]{:S(2)}, u32[]{:S(2)}) async-start(f32[16,32,4,1,128]{4,1,2,3,0:T(8,128)} %bitcast.59), calls=%async_computation.3 | async-start | bytes 2097152 | tf_op jit(solution)/shard_map/all_to_all | solution.py:38
  139.2 38.0 %all-to-all-start.4 = ((f32[16,32,4,1,128]{4,1,2,3,0:T(8,128)}), f32[16,32,4,1,128]{4,1,2,3,0:T(8,128)S(1)}, u32[]{:S(2)}, u32[]{:S(2)}) async-start(f32[16,32,4,1,128]{4,1,2,3,0:T(8,128)} %broadcast_in_dim.17), calls=%async_computation.4 | async-start | bytes 2097152 | tf_op jit(solution)/shard_map/all_to_all | solution.py:50
  146.9 18.9 %collective-permute-start.2 = (f32[32,1,16,128]{3,0,1,2:T(8,128)S(1)}, f32[32,1,16,128]{3,0,1,2:T(8,128)S(1)}, u32[]{:S(2)}, u32[]{:S(2)}) collective-permute-start(f32[32,1,16,128]{3,0,1,2:T(8,128)S(1)} %get-tuple-element.486), channel_id=1, source_target_pairs={{16,0},{32,16},{48,32},{64,48},{80,64},{96,80},{112,96},{128,112},... | collective-permute-start | bytes 786440 | tf_op jit(solution)/shard_map/ppermute | solution.py:67
  156.5 20.8 %collective-permute-start.3 = (f32[32,1,16,128]{3,0,1,2:T(8,128)S(1)}, f32[32,1,16,128]{3,0,1,2:T(8,128)}, u32[]{:S(2)}, u32[]{:S(2)}) collective-permute-start(f32[32,1,16,128]{3,0,1,2:T(8,128)S(1)} %get-tuple-element.485), channel_id=1, source_target_pairs={{0,16},{16,32},{32,48},{48,64},{64,80},{80,96},{96,112},{112,128},... | collective-permute-start | bytes 786440 | tf_op jit(solution)/shard_map/ppermute | solution.py:66
  165.8 0.7 copy-start.3
  181.0 0.7 copy-start.11
  181.0 0.7 copy-start.13
  181.0 0.7 copy-start.15
  224.3 1.0 copy-start.1
